TPU v7x, 512 devices: a whole 4x8x8 slice. The times are simulated.
512 devices in a mesh: tm: 256 (over z, y, x), space: 2 (over core).
Axes of the slice: x: 4, y: 8, z: 8, core: 2. Of those that a mesh axis runs over, the one named last changes fastest.
Arguments:
- image_gradient: bfloat16 [512, 128, 3, 4096], P('tm', 'space'), may hold values from -0.375 to 0.375
- residual: bfloat16 [512, 128, 4096], P('tm', 'space'), may hold values from -6 to 6
- phase: float32 [512], P('tm'), may hold values from 0 to 1
- counts: int32 [128], P('space'), may hold values from 512 to 4096
- owner: int32 [128, 1], P('space'), may hold values from 0 to 1, as said below
Outputs:
- hessian_blocks: float32 [512, 192, 576], P('tm', 'space')
- gradient_blocks: float32 [512, 192, 24], P('tm', 'space')
Inputs may be any that keep to these rules, and one draw needn't show every extreme that they name: Among the 64 bricks of each aligned block at most 48 share an owner, and one owner takes exactly 48 bricks of every block.
All inputs are finite; a program needn't handle non-finite values.
Results may differ from a plain program's by a relative error of at most 0.0029.
Values sent between devices are 32-bit elements; how exact they have to be, the bound alone decides.
A program may use at most 64 MiB of HBM per device.

v0:
```python
import jax
import jax.numpy as jnp
from jax import lax
from jax.sharding import PartitionSpec as P

EDGE = 16


def shifted(block, axis, distance):
    devices = range(lax.axis_size(axis))
    route = [(i - distance, i) for i in devices if i - distance in devices]
    return lax.ppermute(block, axis, route)


def spline_weights(phase):
    return jnp.stack(
        [
            (1.0 - phase) ** 3 / 6.0,
            (3.0 * phase**3 - 6.0 * phase**2 + 4.0) / 6.0,
            (-3.0 * phase**3 + 3.0 * phase**2 + 3.0 * phase + 1.0) / 6.0,
            phase**3 / 6.0,
        ],
        axis=-1,
    )


def shape_table(edge):
    voxel = jnp.arange(edge * edge * edge, dtype=jnp.int32)
    first = ((voxel // (edge * edge)).astype(jnp.float32) + 0.5) / edge
    second = ((voxel // edge % edge).astype(jnp.float32) + 0.5) / edge
    third = ((voxel % edge).astype(jnp.float32) + 0.5) / edge
    rows = []
    for node in range(8):
        along_first = first if node >> 2 & 1 else 1.0 - first
        along_second = second if node >> 1 & 1 else 1.0 - second
        along_third = third if node & 1 else 1.0 - third
        rows.append(along_first * along_second * along_third)
    return jnp.stack(rows, axis=0)


def per_device(image_gradient, residual, phase, counts, owner):
    step_count, brick_count, comp_count, voxel_count = image_gradient.shape
    dof_count = 8 * comp_count
    patch_width = dof_count * dof_count
    column_count = patch_width + dof_count
    first_step = lax.axis_index("tm") * step_count
    overall_step_count = lax.axis_size("tm") * step_count
    space_count = lax.axis_size("space")
    capacity = 3 * brick_count // (2 * space_count)
    valid_mask = lax.broadcasted_iota(jnp.int32, (brick_count, voxel_count), 1) < counts[:, None]
    shapes = shape_table(EDGE)

    def per_step(pair):
        grads, resid = pair
        product = shapes[None, :, None, :] * grads.astype(jnp.float32)[:, None, :, :]
        sens = product.reshape(brick_count, dof_count, voxel_count).astype(jnp.bfloat16)
        masked = jnp.where(valid_mask[:, None, :], sens, jnp.zeros((), jnp.bfloat16))
        hessian = jnp.einsum("bdv,bev->bde", masked, masked, preferred_element_type=jnp.float32)
        gradient = jnp.einsum("bdv,bv->bd", masked, resid, preferred_element_type=jnp.float32)
        return jnp.concatenate([hessian.reshape(brick_count, patch_width), gradient], axis=1)

    patch_contents = lax.map(per_step, (image_gradient, residual))
    weights = spline_weights(phase)
    global_step = first_step + jnp.arange(step_count, dtype=jnp.int32)
    target = jnp.clip(
        global_step[:, None] - 1 + jnp.arange(4, dtype=jnp.int32)[None, :],
        0,
        overall_step_count - 1,
    )
    local_slot = target - first_step + 1
    hits_table = (
        local_slot[:, :, None] == jnp.arange(step_count + 3, dtype=jnp.int32)[None, None, :]
    ).astype(jnp.float32)
    basis_lookup_grid = jnp.sum(weights[:, :, None] * hits_table, axis=1)
    is_hessian_column = (jnp.arange(column_count, dtype=jnp.int32) < patch_width)[None, None, :]
    multiplier = jnp.where(
        is_hessian_column,
        (basis_lookup_grid * basis_lookup_grid)[:, :, None],
        basis_lookup_grid[:, :, None],
    )
    owner_flat = owner[:, 0]
    owner_hits = (owner_flat[:, None] == jnp.arange(space_count, dtype=jnp.int32)[None, :]).astype(
        jnp.int32
    )
    earlier = jnp.cumsum(owner_hits, axis=0) - owner_hits
    brick_rank = jnp.sum(earlier * owner_hits, axis=1)
    destination = owner_flat * capacity + brick_rank
    slot_match = (
        destination[:, None] == jnp.arange(space_count * capacity, dtype=jnp.int32)[None, :]
    )
    source_brick = jnp.sum(
        jnp.where(slot_match, jnp.arange(brick_count, dtype=jnp.int32)[:, None], 0), axis=0
    )
    slot_filled = jnp.any(slot_match, axis=0)
    packed = multiplier[0][:, None, :] * patch_contents[0][None]
    packed = packed + multiplier[1][:, None, :] * patch_contents[1][None]
    from_before = shifted(packed[step_count + 1 :], "tm", 1)
    behind = shifted(packed[:1], "tm", -1)
    own_part = packed[1 : step_count + 1]
    own_part = own_part.at[:2].add(from_before)
    picked = jnp.take(own_part.at[step_count - 1 :].add(behind), source_brick, axis=1)
    placed = jnp.where(slot_filled[None, :, None], picked, jnp.zeros((), jnp.float32))
    result = lax.all_to_all(placed, "space", split_axis=1, concat_axis=1, tiled=True)
    return (result[:, :, :patch_width], result[:, :, patch_width:])


def solution(mesh):
    in_specs = (
        P("tm", "space", None, None),
        P("tm", "space", None),
        P("tm"),
        P("space"),
        P("space", None),
    )
    out_specs = (P("tm", "space", None), P("tm", "space", None))
    return jax.shard_map(
        per_device, mesh=mesh, in_specs=in_specs, out_specs=out_specs, check_vma=False
    )
```

profile of v0, /device:TPU:255, one launch (start us, length us, event | category | flops | bytes accessed | tf_op | source)
XLA Modules:
  0.0 134.0 jit_solution(4634049659191790835)
XLA Ops:
  1.3 102.2 %while.14 = (s32[]{:T(128)}, f32[2,64,600]{1,2,0:T(8,128)}, f32[8,4096]{1,0:T(8,128)S(1)}, bf16[2,64,3,4096]{3,1,2,0:T(8,128)(2,1)}, bf16[2,64,4096]{2,1,0:T(8,128)(2,1)}, /*index=5*/s32[64]{0:T(128)}, s32[]{:T(128)}) while((s32[]{:T(128)}, f32[2,64,600]{1,2,0:T(8,128)}, f32[8,4096]{1,0:T(8,128)S(1)}, ...), condition=%wide.region_6.7_spmd.clone, body=%wide.region_5.6_spmd.clone.sunk | while | flops 334534144 | bytes 58191368 | solution.py:62
  1.3 1.8 %bitcast_convert_fusion.2 = f32[64,3,4096]{2,0,1:T(8,128)S(1)} fusion(bf16[2,64,3,4096]{3,1,2,0:T(8,128)(2,1)} %get-tuple-element.176, s32[]{:T(128)S(6)} %copy.47), kind=kLoop, calls=%fused_computation.9.clone.1 | loop fusion | flops 786432 | bytes 4718596 | tf_op jit(solution)/shard_map/while/body/eval_jaxpr/convert_element_type | solution.py:55
  3.1 0.9 mul.344
  4.0 1.2 mul.345
  5.3 0.2 iota_compare_fusion.6
  5.5 6.0 %fusion.46 = bf16[64,24,4096]{2,0,1:T(8,128)(2,1)} fusion(f32[64,3,4096]{2,0,1:T(8,128)S(1)} %bitcast_convert_fusion.2, f32[24,4096]{1,0:T(8,128)S(1)} %mul.345, pred[64,4096]{1,0:T(8,128)(4,1)S(1)} %iota_compare_fusion.6), kind=kLoop, calls=%fused_computation.4.clone.1 | loop fusion | flops 18874368 | bytes 16384000 | tf_op jit(solution)/shard_map/while/body/eval_jaxpr/jit(_where)/select_n | solution.py:57
  11.6 13.3 %fusion.47 = f32[64,1,24]{2,1,0:T(1,128)S(1)} fusion(bf16[64,24,4096]{2,0,1:T(8,128)(2,1)} %fusion.46, bf16[64,4096,1]{1,0,2:T(8,128)(2,1)S(1)} %dynamic-slice_bitcast_fusion.2), kind=kOutput, calls=%fused_computation.5.clone.1 | convolution fusion | flops 12582912 | bytes 13113344 | tf_op jit(solution)/shard_map/while/body/eval_jaxpr/bdv,bv->bd/dot_general | solution.py:59
  25.0 26.2 %fusion.48 = f32[64,24,24]{2,1,0:T(8,128)S(1)} fusion(bf16[64,24,4096]{2,0,1:T(8,128)(2,1)} %fusion.46), kind=kOutput, calls=%fused_computation.7.clone.1 | convolution fusion | flops 301989888 | bytes 12730368 | tf_op jit(solution)/shard_map/while/body/eval_jaxpr/bdv,bev->bde/dot_general | solution.py:58
  51.2 0.3 copy.43
  51.6 0.8 copy-done.4
  52.4 1.8 %bitcast_convert_fusion.2 = f32[64,3,4096]{2,0,1:T(8,128)S(1)} fusion(bf16[2,64,3,4096]{3,1,2,0:T(8,128)(2,1)} %get-tuple-element.176, s32[]{:T(128)S(6)} %copy.47), kind=kLoop, calls=%fused_computation.9.clone.1 | loop fusion | flops 786432 | bytes 4718596 | tf_op jit(solution)/shard_map/while/body/eval_jaxpr/convert_element_type | solution.py:55
  54.2 0.9 mul.344
  55.1 1.2 mul.345
  56.4 0.2 iota_compare_fusion.6
  56.6 6.0 %fusion.46 = bf16[64,24,4096]{2,0,1:T(8,128)(2,1)} fusion(f32[64,3,4096]{2,0,1:T(8,128)S(1)} %bitcast_convert_fusion.2, f32[24,4096]{1,0:T(8,128)S(1)} %mul.345, pred[64,4096]{1,0:T(8,128)(4,1)S(1)} %iota_compare_fusion.6), kind=kLoop, calls=%fused_computation.4.clone.1 | loop fusion | flops 18874368 | bytes 16384000 | tf_op jit(solution)/shard_map/while/body/eval_jaxpr/jit(_where)/select_n | solution.py:57
  62.7 13.3 %fusion.47 = f32[64,1,24]{2,1,0:T(1,128)S(1)} fusion(bf16[64,24,4096]{2,0,1:T(8,128)(2,1)} %fusion.46, bf16[64,4096,1]{1,0,2:T(8,128)(2,1)S(1)} %dynamic-slice_bitcast_fusion.2), kind=kOutput, calls=%fused_computation.5.clone.1 | convolution fusion | flops 12582912 | bytes 13113344 | tf_op jit(solution)/shard_map/while/body/eval_jaxpr/bdv,bv->bd/dot_general | solution.py:59
  76.1 26.2 %fusion.48 = f32[64,24,24]{2,1,0:T(8,128)S(1)} fusion(bf16[64,24,4096]{2,0,1:T(8,128)(2,1)} %fusion.46), kind=kOutput, calls=%fused_computation.7.clone.1 | convolution fusion | flops 301989888 | bytes 12730368 | tf_op jit(solution)/shard_map/while/body/eval_jaxpr/bdv,bev->bde/dot_general | solution.py:58
  102.3 0.3 copy.43
  102.7 0.8 copy-done.4
  103.5 1.1 slice_bitcast_fusion.1
  105.6 4.3 %collective-permute-start = (f32[2,64,600]{2,0,1:T(2,128)S(1)}, f32[2,64,600]{2,0,1:T(2,128)S(1)}, u32[]{:S(2)}, u32[]{:S(2)}) collective-permute-start(f32[2,64,600]{2,0,1:T(2,128)S(1)} %slice.85), channel_id=1, source_target_pairs={{0,2},{2,4},{4,6},{6,8},{8,10},{10,12},{12,14},{14,16},{16,18},{18... | collective-permute-start | bytes 921608 | tf_op jit(solution)/shard_map/ppermute | solution.py:12
  110.1 1.9 %collective-permute-start.1 = (f32[1,64,600]{2,0,1:T(1,128)S(1)}, f32[1,64,600]{2,0,1:T(1,128)S(1)}, u32[]{:S(2)}, u32[]{:S(2)}) collective-permute-start(f32[1,64,600]{2,0,1:T(1,128)S(1)} %slice.87), channel_id=1, source_target_pairs={{2,0},{4,2},{6,4},{8,6},{10,8},{12,10},{14,12},{16,14},{18,16},{20... | collective-permute-start | bytes 460808 | tf_op jit(solution)/shard_map/ppermute | solution.py:12
  112.6 3.7 %collective-permute-done = f32[2,64,600]{2,0,1:T(2,128)S(1)} collective-permute-done((f32[2,64,600]{2,0,1:T(2,128)S(1)}, f32[2,64,600]{2,0,1:T(2,128)S(1)}, u32[]{:S(2)}, u32[]{:S(2)}) %collective-permute-start) | collective-permute-done | bytes 307232 | tf_op jit(solution)/shard_map/ppermute | solution.py:12
  116.4 0.3 slice_add_fusion
  116.6 5.6 %collective-permute-done.1 = f32[1,64,600]{2,0,1:T(1,128)S(1)} collective-permute-done((f32[1,64,600]{2,0,1:T(1,128)S(1)}, f32[1,64,600]{2,0,1:T(1,128)S(1)}, u32[]{:S(2)}, u32[]{:S(2)}) %collective-permute-start.1) | collective-permute-done | bytes 153632 | tf_op jit(solution)/shard_map/ppermute | solution.py:12
  122.2 0.3 slice_add_fusion.1
  122.5 2.7 %scatter-add.4 = f32[2,64,600]{2,0,1:T(2,128)S(1)} dynamic-update-slice(f32[2,64,600]{2,0,1:T(2,128)S(1)} %slice_add_fusion, f32[1,64,600]{2,0,1:T(1,128)S(1)} %slice_add_fusion.1, s32[]{:T(128)} %constant.202.clone.1, s32[]{:T(128)} %constant.192.clone.1, s32[]{:T(128)} %constant.192.clone.1) | dynamic-update-slice | bytes 307204 | tf_op jit(solution)/shard_map/scatter-add | solution.py:101
  125.2 1.1 gather_fusion
  126.4 0.4 select_bitcast_fusion
  126.7 5.5 %all_to_all.5 = f32[2,96,600]{2,0,1:T(2,128)S(1)} all-to-all(f32[2,96,600]{2,0,1:T(2,128)S(1)} %select_bitcast_fusion), channel_id=1, replica_groups=mesh['tm'=256,'space'=2] {'space'}, dimensions={1} | all-to-all | bytes 921600 | tf_op jit(solution)/shard_map/all_to_all | solution.py:103
  132.3 0.8 copy.24
  133.3 0.7 copy.25
  (63 shorter events, 2.7 us)
Async XLA Ops:
  1.3 103.5 %copy-start.7 = (f32[2]{0:T(128)S(1)}, f32[2]{0:T(128)}, u32[]{:S(2)}) copy-start(f32[2]{0:T(128)} %param.15) | copy-start | bytes 28
  1.3 110.8 %copy-start.6 = (s32[64,1]{0,1:T(1,128)S(1)}, s32[64,1]{0,1:T(1,128)}, u32[]{:S(2)}) copy-start(s32[64,1]{0,1:T(1,128)} %param.17) | copy-start | bytes 772
  1.3 1.8 %copy-start.1 = (f32[8,4096]{1,0:T(8,128)}, f32[8,4096]{1,0:T(8,128)S(1)}, u32[]{:S(2)}) copy-start(f32[8,4096]{1,0:T(8,128)S(1)} %get-tuple-element.175) | copy-start | bytes 393220 | tf_op jit(solution)/shard_map/while
  1.3 4.0 %copy-start.5 = (s32[64]{0:T(128)S(1)}, s32[64]{0:T(128)}, u32[]{:S(2)}) copy-start(s32[64]{0:T(128)} %get-tuple-element.178) | copy-start | bytes 772 | tf_op jit(solution)/shard_map/while
  5.5 6.1 %copy-start = (bf16[2,64,4096]{2,1,0:T(8,128)(2,1)S(1)}, bf16[2,64,4096]{2,1,0:T(8,128)(2,1)}, u32[]{:S(2)}) copy-start(bf16[2,64,4096]{2,1,0:T(8,128)(2,1)} %get-tuple-element.177) | copy-start | bytes 3145732 | tf_op jit(solution)/shard_map/while
  25.0 26.5 %copy-start.3 = (f32[2,64,600]{1,2,0:T(8,128)S(1)}, f32[2,64,600]{1,2,0:T(8,128)}, u32[]{:S(2)}) copy-start(f32[2,64,600]{1,2,0:T(8,128)} %get-tuple-element.167) | copy-start | bytes 921604 | tf_op jit(solution)/shard_map/while
  25.0 27.4 %copy-start.2 = (f32[8,4096]{1,0:T(8,128)S(1)}, f32[8,4096]{1,0:T(8,128)}, u32[]{:S(2)}) copy-start(f32[8,4096]{1,0:T(8,128)} %copy-done.1) | copy-start | bytes 393220 | tf_op jit(solution)/shard_map/while
  51.6 0.9 copy-start.4
  52.4 1.8 %copy-start.1 = (f32[8,4096]{1,0:T(8,128)}, f32[8,4096]{1,0:T(8,128)S(1)}, u32[]{:S(2)}) copy-start(f32[8,4096]{1,0:T(8,128)S(1)} %get-tuple-element.175) | copy-start | bytes 393220 | tf_op jit(solution)/shard_map/while
  52.4 4.0 %copy-start.5 = (s32[64]{0:T(128)S(1)}, s32[64]{0:T(128)}, u32[]{:S(2)}) copy-start(s32[64]{0:T(128)} %get-tuple-element.178) | copy-start | bytes 772 | tf_op jit(solution)/shard_map/while
  56.6 6.1 %copy-start = (bf16[2,64,4096]{2,1,0:T(8,128)(2,1)S(1)}, bf16[2,64,4096]{2,1,0:T(8,128)(2,1)}, u32[]{:S(2)}) copy-start(bf16[2,64,4096]{2,1,0:T(8,128)(2,1)} %get-tuple-element.177) | copy-start | bytes 3145732 | tf_op jit(solution)/shard_map/while
  76.1 26.5 %copy-start.3 = (f32[2,64,600]{1,2,0:T(8,128)S(1)}, f32[2,64,600]{1,2,0:T(8,128)}, u32[]{:S(2)}) copy-start(f32[2,64,600]{1,2,0:T(8,128)} %get-tuple-element.167) | copy-start | bytes 921604 | tf_op jit(solution)/shard_map/while
  76.1 27.4 %copy-start.2 = (f32[8,4096]{1,0:T(8,128)S(1)}, f32[8,4096]{1,0:T(8,128)}, u32[]{:S(2)}) copy-start(f32[8,4096]{1,0:T(8,128)} %copy-done.1) | copy-start | bytes 393220 | tf_op jit(solution)/shard_map/while
  102.7 0.9 copy-start.4
  105.6 10.7 %collective-permute-start = (f32[2,64,600]{2,0,1:T(2,128)S(1)}, f32[2,64,600]{2,0,1:T(2,128)S(1)}, u32[]{:S(2)}, u32[]{:S(2)}) collective-permute-start(f32[2,64,600]{2,0,1:T(2,128)S(1)} %slice.85), channel_id=1, source_target_pairs={{0,2},{2,4},{4,6},{6,8},{8,10},{10,12},{12,14},{14,16},{16,18},{18... | collective-permute-start | bytes 921608 | tf_op jit(solution)/shard_map/ppermute | solution.py:12
  110.1 12.1 %collective-permute-start.1 = (f32[1,64,600]{2,0,1:T(1,128)S(1)}, f32[1,64,600]{2,0,1:T(1,128)S(1)}, u32[]{:S(2)}, u32[]{:S(2)}) collective-permute-start(f32[1,64,600]{2,0,1:T(1,128)S(1)} %slice.87), channel_id=1, source_target_pairs={{2,0},{4,2},{6,4},{8,6},{10,8},{12,10},{14,12},{16,14},{18,16},{20... | collective-permute-start | bytes 460808 | tf_op jit(solution)/shard_map/ppermute | solution.py:12
where the time goes:
time: 134 us
  matrix products  79.1 us (59%)
  other arithmetic  18.4 us (14%)
  local copies, waits for them, and re-layouts  14.3 us (11%)
  waiting for transfers between devices  9.33 us (7%)
  starting transfers between devices  6.25 us (5%)
  blocking collectives  5.55 us (4%)
    dot_general x2, matrix products, per_step(): jnp.einsum('bdv,bev->bde', masked, masked, preferred_element_type=jnp.flo...  52.5 us
    dot_general x2, matrix products, per_step(): jnp.einsum('bdv,bv->bd', masked, resid, preferred_element_type=jnp.float32)  26.7 us
    select_n x2, other arithmetic, per_step(): jnp.where(valid_mask[:, None, :], sens, jnp.zeros((), jnp.bfloat16))  12.1 us
    ppermute x2, waiting for transfers between devices, shifted(): return lax.ppermute(block, axis, route)  9.33 us
    ppermute x2, starting transfers between devices, shifted(): return lax.ppermute(block, axis, route)  6.25 us
    all_to_all x1, blocking collectives, per_device(): lax.all_to_all(placed, 'space', split_axis=1, concat_axis=1, tiled=True)  5.55 us
    mul x4, local copies, waits for them, and re-layouts, per_step(): shapes[None, :, None, :] * grads.astype(jnp.float32)[:, None, :, :]  4.25 us
    convert_element_type x2, other arithmetic, per_step(): grads.astype(jnp.float32)[:, None, :, :]  3.61 us
  transfers between devices with their start and end apart: 2, of which 2 were waited for; matrix products, arithmetic and copies ran while one was open for 1% of the time, Pallas kernels for 0%

commit v1 on v0

--- a/solution.py
+++ b/solution.py
@@ -4,6 +4,19 @@
 from jax.sharding import PartitionSpec as P
 
 EDGE = 16
+
+
+def perform_wires_in(incoming_x, along_dim, ndim_at):
+    kept_arr = jnp.concatenate(
+        lax.all_to_all(
+            jnp.stack(jnp.split(incoming_x, lax.axis_size("space"), along_dim), 0),
+            axis_name="space",
+            split_axis=0,
+            concat_axis=0,
+        ),
+        ndim_at,
+    )
+    return kept_arr
 
 
 def shifted(block, axis, distance):
@@ -100,7 +113,7 @@
     own_part = own_part.at[:2].add(from_before)
     picked = jnp.take(own_part.at[step_count - 1 :].add(behind), source_brick, axis=1)
     placed = jnp.where(slot_filled[None, :, None], picked, jnp.zeros((), jnp.float32))
-    result = lax.all_to_all(placed, "space", split_axis=1, concat_axis=1, tiled=True)
+    result = perform_wires_in(placed, 1, 1)
     return (result[:, :, :patch_width], result[:, :, patch_width:])
 
 

time: 134 us -> 134 us (level)
  no operation moved by 1% of the time
where the time goes in v1:
time: 134 us
  matrix products  79.1 us (59%)
  other arithmetic  18.7 us (14%)
  local copies, waits for them, and re-layouts  13.5 us (10%)
  waiting for transfers between devices  9.33 us (7%)
  starting transfers between devices  6.25 us (5%)
  blocking collectives  5.55 us (4%)
    dot_general x2, matrix products, per_step(): jnp.einsum('bdv,bev->bde', masked, masked, preferred_element_type=jnp.flo...  52.5 us
    dot_general x2, matrix products, per_step(): jnp.einsum('bdv,bv->bd', masked, resid, preferred_element_type=jnp.float32)  26.7 us
    select_n x2, other arithmetic, per_step(): jnp.where(valid_mask[:, None, :], sens, jnp.zeros((), jnp.bfloat16))  12.2 us
    ppermute x2, waiting for transfers between devices, shifted(): return lax.ppermute(block, axis, route)  9.33 us
    ppermute x2, starting transfers between devices, shifted(): return lax.ppermute(block, axis, route)  6.25 us
    all_to_all x1, blocking collectives, perform_wires_in(): lax.all_to_all(jnp.stack(jnp.split(incoming_x, lax.axis_size('space'), al...  5.55 us
    mul x4, local copies, waits for them, and re-layouts, per_step(): shapes[None, :, None, :] * grads.astype(jnp.float32)[:, None, :, :]  4.24 us
    convert_element_type x2, other arithmetic, per_step(): grads.astype(jnp.float32)[:, None, :, :]  3.61 us
  transfers between devices with their start and end apart: 2, of which 2 were waited for; matrix products, arithmetic and copies ran while one was open for 1% of the time, Pallas kernels for 0%

profile of v1, /device:TPU:255, one launch (start us, length us, event | category | flops | bytes accessed | tf_op | source)
XLA Modules:
  0.0 133.5 jit_solution(3300866078315685001)
XLA Ops:
  1.3 102.3 %while.14 = (s32[]{:T(128)}, f32[2,64,600]{1,2,0:T(8,128)}, f32[8,4096]{1,0:T(8,128)S(1)}, bf16[2,64,3,4096]{3,1,2,0:T(8,128)(2,1)}, bf16[2,64,4096]{2,1,0:T(8,128)(2,1)}, /*index=5*/s32[64]{0:T(128)}, s32[]{:T(128)}) while((s32[]{:T(128)}, f32[2,64,600]{1,2,0:T(8,128)}, f32[8,4096]{1,0:T(8,128)S(1)}, ...), condition=%wide.region_6.7_spmd.clone, body=%wide.region_5.6_spmd.clone.sunk | while | flops 334534144 | bytes 58191368 | solution.py:75
  1.3 1.8 %bitcast_convert_fusion.2 = f32[64,3,4096]{2,0,1:T(8,128)S(1)} fusion(bf16[2,64,3,4096]{3,1,2,0:T(8,128)(2,1)} %get-tuple-element.178, s32[]{:T(128)S(6)} %copy.48), kind=kLoop, calls=%fused_computation.9.clone.1 | loop fusion | flops 786432 | bytes 4718596 | tf_op jit(solution)/shard_map/while/body/eval_jaxpr/convert_element_type | solution.py:68
  3.1 0.9 mul.344
  4.0 1.2 mul.345
  5.3 0.2 iota_compare_fusion.6
  5.5 6.1 %fusion.46 = bf16[64,24,4096]{2,0,1:T(8,128)(2,1)} fusion(f32[64,3,4096]{2,0,1:T(8,128)S(1)} %bitcast_convert_fusion.2, f32[24,4096]{1,0:T(8,128)S(1)} %mul.345, pred[64,4096]{1,0:T(8,128)(4,1)S(1)} %iota_compare_fusion.6), kind=kLoop, calls=%fused_computation.4.clone.1 | loop fusion | flops 18874368 | bytes 16384000 | tf_op jit(solution)/shard_map/while/body/eval_jaxpr/jit(_where)/select_n | solution.py:70
  11.6 13.3 %fusion.47 = f32[64,1,24]{2,1,0:T(1,128)S(1)} fusion(bf16[64,24,4096]{2,0,1:T(8,128)(2,1)} %fusion.46, bf16[64,4096,1]{1,0,2:T(8,128)(2,1)S(1)} %dynamic-slice_bitcast_fusion.2), kind=kOutput, calls=%fused_computation.5.clone.1 | convolution fusion | flops 12582912 | bytes 13113344 | tf_op jit(solution)/shard_map/while/body/eval_jaxpr/bdv,bv->bd/dot_general | solution.py:72
  25.0 26.2 %fusion.48 = f32[64,24,24]{2,1,0:T(8,128)S(1)} fusion(bf16[64,24,4096]{2,0,1:T(8,128)(2,1)} %fusion.46), kind=kOutput, calls=%fused_computation.7.clone.1 | convolution fusion | flops 301989888 | bytes 12730368 | tf_op jit(solution)/shard_map/while/body/eval_jaxpr/bdv,bev->bde/dot_general | solution.py:71
  51.3 0.3 copy.44
  51.6 0.8 copy-done.5
  52.4 1.8 %bitcast_convert_fusion.2 = f32[64,3,4096]{2,0,1:T(8,128)S(1)} fusion(bf16[2,64,3,4096]{3,1,2,0:T(8,128)(2,1)} %get-tuple-element.178, s32[]{:T(128)S(6)} %copy.48), kind=kLoop, calls=%fused_computation.9.clone.1 | loop fusion | flops 786432 | bytes 4718596 | tf_op jit(solution)/shard_map/while/body/eval_jaxpr/convert_element_type | solution.py:68
  54.3 0.9 mul.344
  55.2 1.2 mul.345
  56.4 0.2 iota_compare_fusion.6
  56.6 6.1 %fusion.46 = bf16[64,24,4096]{2,0,1:T(8,128)(2,1)} fusion(f32[64,3,4096]{2,0,1:T(8,128)S(1)} %bitcast_convert_fusion.2, f32[24,4096]{1,0:T(8,128)S(1)} %mul.345, pred[64,4096]{1,0:T(8,128)(4,1)S(1)} %iota_compare_fusion.6), kind=kLoop, calls=%fused_computation.4.clone.1 | loop fusion | flops 18874368 | bytes 16384000 | tf_op jit(solution)/shard_map/while/body/eval_jaxpr/jit(_where)/select_n | solution.py:70
  62.8 13.3 %fusion.47 = f32[64,1,24]{2,1,0:T(1,128)S(1)} fusion(bf16[64,24,4096]{2,0,1:T(8,128)(2,1)} %fusion.46, bf16[64,4096,1]{1,0,2:T(8,128)(2,1)S(1)} %dynamic-slice_bitcast_fusion.2), kind=kOutput, calls=%fused_computation.5.clone.1 | convolution fusion | flops 12582912 | bytes 13113344 | tf_op jit(solution)/shard_map/while/body/eval_jaxpr/bdv,bv->bd/dot_general | solution.py:72
  76.2 26.2 %fusion.48 = f32[64,24,24]{2,1,0:T(8,128)S(1)} fusion(bf16[64,24,4096]{2,0,1:T(8,128)(2,1)} %fusion.46), kind=kOutput, calls=%fused_computation.7.clone.1 | convolution fusion | flops 301989888 | bytes 12730368 | tf_op jit(solution)/shard_map/while/body/eval_jaxpr/bdv,bev->bde/dot_general | solution.py:71
  102.4 0.3 copy.44
  102.7 0.8 copy-done.5
  103.6 1.1 slice_bitcast_fusion.1
  105.7 4.3 %collective-permute-start = (f32[2,64,600]{2,0,1:T(2,128)S(1)}, f32[2,64,600]{2,0,1:T(2,128)S(1)}, u32[]{:S(2)}, u32[]{:S(2)}) collective-permute-start(f32[2,64,600]{2,0,1:T(2,128)S(1)} %slice.85), channel_id=1, source_target_pairs={{0,2},{2,4},{4,6},{6,8},{8,10},{10,12},{12,14},{14,16},{16,18},{18... | collective-permute-start | bytes 921608 | tf_op jit(solution)/shard_map/ppermute | solution.py:25
  110.2 1.9 %collective-permute-start.1 = (f32[1,64,600]{2,0,1:T(1,128)S(1)}, f32[1,64,600]{2,0,1:T(1,128)S(1)}, u32[]{:S(2)}, u32[]{:S(2)}) collective-permute-start(f32[1,64,600]{2,0,1:T(1,128)S(1)} %slice.87), channel_id=1, source_target_pairs={{2,0},{4,2},{6,4},{8,6},{10,8},{12,10},{14,12},{16,14},{18,16},{20... | collective-permute-start | bytes 460808 | tf_op jit(solution)/shard_map/ppermute | solution.py:25
  112.7 3.7 %collective-permute-done = f32[2,64,600]{2,0,1:T(2,128)S(1)} collective-permute-done((f32[2,64,600]{2,0,1:T(2,128)S(1)}, f32[2,64,600]{2,0,1:T(2,128)S(1)}, u32[]{:S(2)}, u32[]{:S(2)}) %collective-permute-start) | collective-permute-done | bytes 307232 | tf_op jit(solution)/shard_map/ppermute | solution.py:25
  116.4 0.3 slice_add_fusion
  116.7 5.6 %collective-permute-done.1 = f32[1,64,600]{2,0,1:T(1,128)S(1)} collective-permute-done((f32[1,64,600]{2,0,1:T(1,128)S(1)}, f32[1,64,600]{2,0,1:T(1,128)S(1)}, u32[]{:S(2)}, u32[]{:S(2)}) %collective-permute-start.1) | collective-permute-done | bytes 153632 | tf_op jit(solution)/shard_map/ppermute | solution.py:25
  122.3 0.3 slice_add_fusion.1
  122.5 2.7 %scatter-add.4 = f32[2,64,600]{2,0,1:T(2,128)S(1)} dynamic-update-slice(f32[2,64,600]{2,0,1:T(2,128)S(1)} %slice_add_fusion, f32[1,64,600]{2,0,1:T(1,128)S(1)} %slice_add_fusion.1, s32[]{:T(128)} %constant.202.clone.1, s32[]{:T(128)} %constant.192.clone.1, s32[]{:T(128)} %constant.192.clone.1) | dynamic-update-slice | bytes 307204 | tf_op jit(solution)/shard_map/scatter-add | solution.py:114
  125.3 1.1 gather_fusion
  126.4 0.4 select_bitcast_fusion
  126.9 0.2 pad_maximum_fusion
  127.1 5.5 %all_to_all.5 = f32[2,2,48,600]{3,1,2,0:T(2,128)S(1)} all-to-all(f32[2,2,48,600]{3,1,2,0:T(2,128)S(1)} %pad_maximum_fusion), channel_id=1, replica_groups=mesh['tm'=256,'space'=2] {'space'}, dimensions={0} | all-to-all | bytes 921600 | tf_op jit(solution)/shard_map/all_to_all | solution.py:11
  132.8 0.7 copy.26
  (67 shorter events, 2.8 us)
Async XLA Ops:
  1.3 103.6 %copy-start.8 = (f32[2]{0:T(128)S(1)}, f32[2]{0:T(128)}, u32[]{:S(2)}) copy-start(f32[2]{0:T(128)} %param.15) | copy-start | bytes 28
  1.3 110.8 %copy-start.7 = (s32[64,1]{0,1:T(1,128)S(1)}, s32[64,1]{0,1:T(1,128)}, u32[]{:S(2)}) copy-start(s32[64,1]{0,1:T(1,128)} %param.17) | copy-start | bytes 772
  1.3 1.8 %copy-start.1 = (f32[8,4096]{1,0:T(8,128)}, f32[8,4096]{1,0:T(8,128)S(1)}, u32[]{:S(2)}) copy-start(f32[8,4096]{1,0:T(8,128)S(1)} %get-tuple-element.177) | copy-start | bytes 393220 | tf_op jit(solution)/shard_map/while
  1.3 4.0 %copy-start.6 = (s32[64]{0:T(128)S(1)}, s32[64]{0:T(128)}, u32[]{:S(2)}) copy-start(s32[64]{0:T(128)} %get-tuple-element.180) | copy-start | bytes 772 | tf_op jit(solution)/shard_map/while
  5.5 6.1 %copy-start = (bf16[2,64,4096]{2,1,0:T(8,128)(2,1)S(1)}, bf16[2,64,4096]{2,1,0:T(8,128)(2,1)}, u32[]{:S(2)}) copy-start(bf16[2,64,4096]{2,1,0:T(8,128)(2,1)} %get-tuple-element.179) | copy-start | bytes 3145732 | tf_op jit(solution)/shard_map/while
  25.0 26.5 %copy-start.4 = (f32[2,64,600]{1,2,0:T(8,128)S(1)}, f32[2,64,600]{1,2,0:T(8,128)}, u32[]{:S(2)}) copy-start(f32[2,64,600]{1,2,0:T(8,128)} %get-tuple-element.169) | copy-start | bytes 921604 | tf_op jit(solution)/shard_map/while
  25.0 27.4 %copy-start.2 = (f32[8,4096]{1,0:T(8,128)S(1)}, f32[8,4096]{1,0:T(8,128)}, u32[]{:S(2)}) copy-start(f32[8,4096]{1,0:T(8,128)} %copy-done.1) | copy-start | bytes 393220 | tf_op jit(solution)/shard_map/while
  51.6 0.8 copy-start.5
  52.4 1.8 %copy-start.1 = (f32[8,4096]{1,0:T(8,128)}, f32[8,4096]{1,0:T(8,128)S(1)}, u32[]{:S(2)}) copy-start(f32[8,4096]{1,0:T(8,128)S(1)} %get-tuple-element.177) | copy-start | bytes 393220 | tf_op jit(solution)/shard_map/while
  52.4 4.0 %copy-start.6 = (s32[64]{0:T(128)S(1)}, s32[64]{0:T(128)}, u32[]{:S(2)}) copy-start(s32[64]{0:T(128)} %get-tuple-element.180) | copy-start | bytes 772 | tf_op jit(solution)/shard_map/while
  56.6 6.1 %copy-start = (bf16[2,64,4096]{2,1,0:T(8,128)(2,1)S(1)}, bf16[2,64,4096]{2,1,0:T(8,128)(2,1)}, u32[]{:S(2)}) copy-start(bf16[2,64,4096]{2,1,0:T(8,128)(2,1)} %get-tuple-element.179) | copy-start | bytes 3145732 | tf_op jit(solution)/shard_map/while
  76.2 26.5 %copy-start.4 = (f32[2,64,600]{1,2,0:T(8,128)S(1)}, f32[2,64,600]{1,2,0:T(8,128)}, u32[]{:S(2)}) copy-start(f32[2,64,600]{1,2,0:T(8,128)} %get-tuple-element.169) | copy-start | bytes 921604 | tf_op jit(solution)/shard_map/while
  76.2 27.4 %copy-start.2 = (f32[8,4096]{1,0:T(8,128)S(1)}, f32[8,4096]{1,0:T(8,128)}, u32[]{:S(2)}) copy-start(f32[8,4096]{1,0:T(8,128)} %copy-done.1) | copy-start | bytes 393220 | tf_op jit(solution)/shard_map/while
  102.7 0.8 copy-start.5
  105.7 10.7 %collective-permute-start = (f32[2,64,600]{2,0,1:T(2,128)S(1)}, f32[2,64,600]{2,0,1:T(2,128)S(1)}, u32[]{:S(2)}, u32[]{:S(2)}) collective-permute-start(f32[2,64,600]{2,0,1:T(2,128)S(1)} %slice.85), channel_id=1, source_target_pairs={{0,2},{2,4},{4,6},{6,8},{8,10},{10,12},{12,14},{14,16},{16,18},{18... | collective-permute-start | bytes 921608 | tf_op jit(solution)/shard_map/ppermute | solution.py:25
  110.2 12.1 %collective-permute-start.1 = (f32[1,64,600]{2,0,1:T(1,128)S(1)}, f32[1,64,600]{2,0,1:T(1,128)S(1)}, u32[]{:S(2)}, u32[]{:S(2)}) collective-permute-start(f32[1,64,600]{2,0,1:T(1,128)S(1)} %slice.87), channel_id=1, source_target_pairs={{2,0},{4,2},{6,4},{8,6},{10,8},{12,10},{14,12},{16,14},{18,16},{20... | collective-permute-start | bytes 460808 | tf_op jit(solution)/shard_map/ppermute | solution.py:25
  132.7 0.8 copy-start.3
